TPU v7x, 1024 devices: a whole 4x8x16 slice. The times are simulated.
1024 devices in a mesh: lev: 16 (over x_lo, y), lat: 64 (over z, x_hi, core).
Axes of the slice: x: 4 (x_hi: 2, x_lo: 2; x = x_hi * 2 + x_lo), y: 8, z: 16, core: 2. Of those that a mesh axis runs over, the one named last changes fastest.
Arguments:
- state: float32 [4, 128, 192, 1024], P(None, 'lev', 'lat'), may hold values from -6 to 6
- wind_east: float32 [128, 192, 1024], P('lev', 'lat'), may hold values from -0.45 to 0.45
- wind_north: float32 [128, 192, 1024], P('lev', 'lat'), may hold values from -0.45 to 0.45
- remap_weight: float32 [128, 128], replicated, may hold values from 0.05 to 1
- block_list: int32 [16, 64, 8], P('lev', 'lat'), may hold values from 0 to 7, as said below
- block_count: int32 [16, 64], P('lev', 'lat'), may hold values from 0 to 8, as said below
- w_in: bfloat16 [512, 1024], replicated, may hold values from -1 to 1
- w_mid: bfloat16 [1024, 1024], replicated, may hold values from -0.1875 to 0.1875
- w_out: bfloat16 [1024, 512], replicated, may hold values from -0.375 to 0.375
Outputs:
- new_state: float32 [4, 128, 192, 1024], P(None, 'lev', 'lat')
Inputs may be any that keep to these rules, and one draw needn't show every extreme that they name: Each row block_list[m, g, :] names every block 0 to 7 exactly once. block_count[m, g] + block_count[m, (g + 32) mod 64] equals 8 for every m and g; some entry equals 8.
All inputs are finite; a program needn't handle non-finite values.
Results may differ from a plain program's by a relative error of at most 0.0045.
Values may be sent and summed in bfloat16 or wider, within the bound.
No kernel may reach another device: no remote copies, remote signals or barrier semaphores. Data moves between devices by JAX's collectives and lax.ppermute only.
A program may use at most 32 MiB of HBM per device.

v0:
```python
import jax
import jax.numpy as jnp
from jax import lax
from jax.experimental import pallas as pl
from jax.experimental.pallas import tpu as pltpu
from jax.sharding import PartitionSpec as P


F32 = jnp.float32
BF16 = jnp.bfloat16
VM = pltpu.VMEM


def whole():
    return pl.BlockSpec(memory_space=VM)


def in_hbm(array):
    return pltpu.with_memory_space_constraint(array, pltpu.HBM)


def cost(flops, moved):
    return pl.CostEstimate(flops=flops, bytes_accessed=moved, transcendentals=0)


def params(mib):
    return pltpu.CompilerParams(vmem_limit_bytes=mib * 2**20)


def even_band():
    return lax.rem(lax.axis_index("lat"), 2) == 0


def edge_kernel(state_ref, north_ref, near_ref, far_ref, rows_ref, winds_ref, sems):
    fields, rows = state_ref.shape[:2]
    last = rows - 1
    even = even_band()
    near_row = jnp.where(even, last, 0)
    copies = []
    for k, row in enumerate((last - near_row, near_row)):
        for source, target, sem in (
            (state_ref.at[:, row], rows_ref.at[k], sems.at[k, 0]),
            (north_ref.at[row], winds_ref.at[k], sems.at[k, 1]),
        ):
            copy = pltpu.make_async_copy(source, target, sem)
            copy.start()
            copies.append(copy)
    for copy in copies:
        copy.wait()
    for k, edge_ref in enumerate((far_ref, near_ref)):
        for f in range(fields):
            edge_ref[f] = rows_ref[k, f].astype(BF16)
        edge_ref[fields] = winds_ref[k].astype(BF16)


def pair_remap(weight):
    n = weight.shape[0]
    row = lax.broadcasted_iota(jnp.int32, (n, n), 0)
    col = lax.broadcasted_iota(jnp.int32, (n, n), 1)
    raw = weight + jnp.where(row == col, 16.0, 0.0)
    remap = (raw / jnp.sum(raw, axis=1, keepdims=True)).T
    zero = jnp.zeros((8, n), F32)
    rows = []
    for m in range(n // 8):
        piece = remap[m * 8 : (m + 1) * 8]
        rows.append(jnp.concatenate([piece, zero], axis=1))
        rows.append(jnp.concatenate([zero, piece], axis=1))
    return jnp.concatenate(rows, axis=0)


def upwind(wind, cells, beyond):
    return wind * jnp.where(wind > 0.0, cells, beyond)


def local_kernel(
    state_ref, east_ref, north_ref, list_ref, count_ref, weight_ref,
    out_ref, high_ref, low_ref, mask_ref,
):
    fields, rows, _, width = state_ref.shape

    def field(f, carry):
        below_flux = None
        for j in range(rows):
            cells = state_ref[f, j]
            wind = north_ref[j]
            easterly = east_ref[j]
            east_cells = pltpu.roll(cells, width - 1, 1)
            east_flux = upwind(easterly, cells, east_cells)
            west_flux = pltpu.roll(east_flux, 1, 1)
            value = cells - (east_flux - west_flux)
            if below_flux is not None:
                value = value + below_flux
            if j < rows - 1:
                below_flux = upwind(wind, cells, state_ref[f, j + 1])
                value = value - below_flux
            out_ref[f, j] = value
        return carry

    lax.fori_loop(0, fields, field, 0)
    pair = pair_remap(weight_ref[...])
    high = pair.astype(BF16)
    high_ref[...] = high
    low_ref[...] = (pair - high.astype(F32)).astype(BF16)
    odd = lax.rem(lax.axis_index("lev"), 2)
    place = lax.broadcasted_iota(jnp.int32, mask_ref.shape, 0)
    column = jnp.where(place < 128, place + 64 * odd, place - 128 * odd)
    block = jnp.right_shift(column * 2731, 16)
    names = list_ref[0]
    slot = lax.broadcasted_iota(jnp.int32, names.shape, 1)
    marks = jnp.where(slot < count_ref[:, :1], jnp.left_shift(jnp.int32(1), names), 0)
    bits = jnp.sum(marks.astype(F32), axis=1, keepdims=True).astype(jnp.int32)
    active = jnp.bitwise_and(jnp.right_shift(bits, block), 1).astype(F32)
    mask_ref[...] = active


def finish_kernel(local_ref, state_ref, north_ref, near_ref, far_ref, out_ref):
    fields, rows = state_ref.shape[:2]
    last = rows - 1
    wall = lax.axis_index("lat") == lax.axis_size("lat") - 1
    wind = north_ref[last] * jnp.where(wall, 0.0, 1.0).astype(F32)
    even = even_band()

    def edge(first, second, f):
        return jnp.where(even, first[f].astype(F32), second[f].astype(F32))

    wind_below = edge(far_ref, near_ref, fields)
    low = lax.broadcasted_iota(jnp.int32, (8, 128), 1) < 64
    updated = []
    for f in range(fields):
        south = upwind(wind_below, edge(far_ref, near_ref, f), state_ref[f, 0])
        north = upwind(wind, state_ref[f, last], edge(near_ref, far_ref, f))
        pieces = [local_ref[f, j] for j in range(rows)]
        pieces[0] = pieces[0] + south
        pieces[last] = pieces[last] - north
        updated.append(pieces)

    def tile(f, v):
        j, k = divmod(v, 8)
        return updated[f][j][:, k * 128 : (k + 1) * 128]

    for p in range(8):
        full_a = [tile(f, 3 * p) for f in range(fields)]
        half = [tile(f, 3 * p + 1) for f in range(fields)]
        full_b = [tile(f, 3 * p + 2) for f in range(fields)]
        turned = [pltpu.roll(h, 64, 1) for h in half]
        half_a = [jnp.where(low, half[f], turned[f + 2]) for f in range(2)]
        half_b = [jnp.where(low, turned[f], half[f + 2]) for f in range(2)]
        out_ref[2 * p] = jnp.concatenate(full_a + half_a, axis=0).astype(BF16)
        out_ref[2 * p + 1] = jnp.concatenate(full_b + half_b, axis=0).astype(BF16)


def silu(v):
    return v / (1.0 + jnp.exp(-v))


def physics_kernel(
    data_ref, high_ref, low_ref, mask_ref, w_in_ref, w_mid_ref, w_out_ref, out_ref
):
    def turned(r):
        block = data_ref[:, r : r + 16, :].reshape(256, 128)
        return block.T

    ends = turned(32)
    x = []
    for p in range(2):
        cols = jnp.concatenate([turned(16 * p), ends[64 * p : 64 * p + 64]], axis=0)
        x.append(
            jnp.dot(cols, high_ref[...], preferred_element_type=F32)
            + jnp.dot(cols, low_ref[...], preferred_element_type=F32)
        )
    remapped = jnp.concatenate(x, axis=1)
    first = silu(jnp.dot(remapped.astype(BF16), w_in_ref[...], preferred_element_type=F32)).astype(BF16)
    second = silu(jnp.dot(first, w_mid_ref[...], preferred_element_type=F32)).astype(BF16)
    tendency = jnp.dot(second, w_out_ref[...], preferred_element_type=F32)
    active = jnp.concatenate([mask_ref[...]] * 4, axis=1) > 0.0
    finished = remapped + jnp.where(active, tendency, 0.0)

    def put(r, rows):
        back = rows.T.reshape(2, 16, 8, 128)
        both = jnp.concatenate([back[0], back[1]], axis=1)
        out_ref[:, r : r + 16, :] = both.astype(BF16)

    put(0, finished[:128, :256])
    put(16, finished[:128, 256:])
    put(32, jnp.concatenate([finished[128:, :256], finished[128:, 256:]], axis=0))


def unpack_kernel(data_ref, out_ref, buffer, sems):
    fields = out_ref.shape[0]
    low = lax.broadcasted_iota(jnp.int32, (16, 128), 1) < 64
    copies = []
    for pair in range(fields // 2):

        def put(v, value):
            j, k = divmod(v, 8)
            for f in range(2):
                buffer[2 * pair + f, j, :, k * 128 : (k + 1) * 128] = value[8 * f : 8 * f + 8]

        for p in range(8):
            put(3 * p, data_ref[2 * p, 16 * pair : 16 * pair + 16].astype(F32))
            put(3 * p + 2, data_ref[2 * p + 1, 16 * pair : 16 * pair + 16].astype(F32))
            end_a, end_b = (data_ref[2 * p + i, 32:].astype(F32) for i in range(2))
            if pair == 0:
                put(3 * p + 1, jnp.where(low, end_a, pltpu.roll(end_b, 64, 1)))
            else:
                put(3 * p + 1, jnp.where(low, pltpu.roll(end_a, 64, 1), end_b))
        ready = pl.ds(2 * pair, 2)
        copy = pltpu.make_async_copy(buffer.at[ready], out_ref.at[ready], sems.at[pair])
        copy.start()
        copies.append(copy)
    for copy in copies:
        copy.wait()


def pairs(start, count):
    lower = range(start, count - 1, 2)
    return [(i, i + 1) for i in lower] + [(i + 1, i) for i in lower]


def per_device(
    state, wind_east, wind_north, remap_weight, block_list, block_count, w_in, w_mid, w_out
):
    fields, lev_dev, lat_rows, lon_cells = state.shape
    lev_count = lax.axis_size("lev")
    lat_count = lax.axis_size("lat")
    cells = jnp.transpose(state, (0, 2, 1, 3))
    east = jnp.transpose(wind_east, (1, 0, 2))
    north = jnp.transpose(wind_north, (1, 0, 2))
    edge = (lev_dev, lon_cells)
    hbm = pl.BlockSpec(memory_space=pltpu.HBM)
    levels = lev_dev * lev_count
    col_count = lat_rows * lon_cells // lev_count
    near, far = pl.pallas_call(
        edge_kernel,
        out_shape=[jax.ShapeDtypeStruct((fields + 1, *edge), BF16)] * 2,
        in_specs=[hbm] * 2,
        out_specs=[whole()] * 2,
        scratch_shapes=[
            VM((2, fields, *edge), F32),
            VM((2, *edge), F32),
            pltpu.SemaphoreType.DMA((2, 2)),
        ],
        compiler_params=params(4),
        cost_estimate=cost(1 << 33, 1 << 21),
        name="edges",
    )(*map(in_hbm, (cells, north)))
    far = lax.ppermute(far, "lat", pairs(1, lat_count))
    near = lax.ppermute(near, "lat", pairs(0, lat_count))
    local, high, low, mask = pl.pallas_call(
        local_kernel,
        out_shape=[
            jax.ShapeDtypeStruct(cells.shape, F32),
            jax.ShapeDtypeStruct((2 * levels, 2 * levels), BF16),
            jax.ShapeDtypeStruct((2 * levels, 2 * levels), BF16),
            jax.ShapeDtypeStruct((col_count, 128), F32),
        ],
        in_specs=[whole()] * 6,
        out_specs=[whole()] * 4,
        compiler_params=params(4),
        cost_estimate=cost(1 << 22, 1 << 22),
        name="local",
    )(cells, east, north, block_list, lax.pad(block_count, jnp.int32(0), ((0, 0, 0), (0, 127, 0))), remap_weight)
    chunk = (lev_count, fields * lev_dev * lat_rows * lon_cells // lev_count // 128, 128)
    packed = pl.pallas_call(
        finish_kernel,
        out_shape=jax.ShapeDtypeStruct(chunk, BF16),
        in_specs=[whole()] * 5,
        out_specs=whole(),
        compiler_params=params(4),
        cost_estimate=cost(1 << 34, 1 << 20),
        name="finish",
    )(local, cells, north, near, far)
    packed, high, low, mask = lax.optimization_barrier((packed, high, low, mask))
    columns = lax.all_to_all(packed, "lev", split_axis=0, concat_axis=0, tiled=True)
    finished = pl.pallas_call(
        physics_kernel,
        out_shape=jax.ShapeDtypeStruct(chunk, BF16),
        in_specs=[whole()] * 7,
        out_specs=whole(),
        compiler_params=params(16),
        cost_estimate=cost(1 << 30, 1 << 22),
        name="physics",
    )(columns, high, low, mask, w_in, w_mid, w_out)
    returned = lax.all_to_all(finished, "lev", split_axis=0, concat_axis=0, tiled=True)
    result = pl.pallas_call(
        unpack_kernel,
        out_shape=jax.ShapeDtypeStruct(cells.shape, F32),
        in_specs=[whole()],
        out_specs=hbm,
        scratch_shapes=[VM(cells.shape, F32), pltpu.SemaphoreType.DMA((2,))],
        compiler_params=params(4),
        cost_estimate=cost(1 << 18, 1 << 20),
        name="unpack",
    )(returned)
    return jnp.transpose(result, (0, 2, 1, 3))


def solution(mesh):
    placed = (
        P(None, "lev", "lat", None),
        P("lev", "lat", None),
        P("lev", "lat", None),
        P(),
        P("lev", "lat", None),
        P("lev", "lat"),
        P(),
        P(),
        P(),
    )
    return jax.shard_map(
        per_device,
        mesh=mesh,
        in_specs=placed,
        out_specs=P(None, "lev", "lat", None),
        check_vma=False,
    )
```

profile of v0, /device:TPU:1, one launch (start us, length us, event | category | flops | bytes accessed | tf_op | source)
XLA Modules:
  0.0 48.2 jit_solution(8905544577850769483)
XLA Ops:
  0.0 0.0 copy-start.3
  0.0 0.0 copy-start.4
  0.0 0.0 copy-start.5
  0.0 0.0 copy-start.6
  0.0 0.0 copy-start.7
  0.0 1.1 %edges.1 = (bf16[5,8,1024]{2,1,0:T(8,128)(2,1)S(1)}, bf16[5,8,1024]{2,1,0:T(8,128)(2,1)S(1)}) custom-call(f32[4,3,8,1024]{3,2,1,0:T(8,128)} %bitcast.4, f32[3,8,1024]{2,1,0:T(8,128)} %bitcast.8), custom_call_target="tpu_custom_call" | custom-call | flops 8589934592 | bytes 2097152 | tf_op jit(solution)/shard_map/edges/pallas_call | solution.py:233
  1.1 16.0 %collective-permute-start = (bf16[5,8,1024]{2,1,0:T(8,128)(2,1)S(1)}, bf16[5,8,1024]{2,1,0:T(8,128)(2,1)S(1)}, u32[]{:S(2)}, u32[]{:S(2)}) collective-permute-start(bf16[5,8,1024]{2,1,0:T(8,128)(2,1)S(1)} %get-tuple-element.16), channel_id=1, source_target_pairs={{0,1},{2,3},{4,5},{6,7},{8,9},{10,11},{12,13},{14,15},{16,17},{18,... | collective-permute-start | bytes 245768 | tf_op jit(solution)/shard_map/ppermute | solution.py:248
  17.2 1.9 %collective-permute-start.1 = (bf16[5,8,1024]{2,1,0:T(8,128)(2,1)S(1)}, bf16[5,8,1024]{2,1,0:T(8,128)(2,1)S(1)}, u32[]{:S(2)}, u32[]{:S(2)}) collective-permute-start(bf16[5,8,1024]{2,1,0:T(8,128)(2,1)S(1)} %get-tuple-element.17), channel_id=1, source_target_pairs={{1,2},{3,4},{5,6},{7,8},{9,10},{11,12},{13,14},{15,16},{17,18},{19... | collective-permute-start | bytes 245768 | tf_op jit(solution)/shard_map/ppermute | solution.py:247
  19.8 0.0 copy-done.3
  19.8 0.0 copy-done.4
  19.8 0.0 copy-done.5
  19.8 0.0 copy-done.6
  19.8 0.0 copy-done.7
  19.8 0.9 %local.1 = (f32[4,3,8,1024]{3,2,1,0:T(8,128)S(1)}, bf16[256,256]{1,0:T(8,128)(2,1)S(1)}, bf16[256,256]{1,0:T(8,128)(2,1)S(1)}, f32[192,128]{1,0:T(8,128)S(1)}) custom-call(f32[4,3,8,1024]{3,2,1,0:T(8,128)S(1)} %bitcast.5, f32[3,8,1024]{2,1,0:T(8,128)S(1)} %bitcast.7, f32[3,8,1024]{2,1,0:T(8,128)S(1)} %bitcast.9, s32[1,1,8]{2,1,0:T(1,128)S(1)} %copy-done.7, ...), custom_call_target="tpu_custom_call" | custom-call | flops 4194304 | bytes 4194304 | tf_op jit(solution)/shard_map/local/pallas_call | solution.py:249
  20.7 0.0 collective-permute-done.near_ref
  20.7 3.8 %collective-permute-done.1.far_ref = bf16[5,8,1024]{2,1,0:T(8,128)(2,1)S(1)} collective-permute-done((bf16[5,8,1024]{2,1,0:T(8,128)(2,1)S(1)}, bf16[5,8,1024]{2,1,0:T(8,128)(2,1)S(1)}, u32[]{:S(2)}, u32[]{:S(2)}) %collective-permute-start.1) | collective-permute-done | bytes 81952 | tf_op jit(solution)/shard_map/ppermute | solution.py:247
  24.6 0.0 copy-start
  24.6 0.0 copy-start.1
  24.6 0.0 copy-start.2
  24.6 0.1 finish.1
  24.7 10.3 %all_to_all.10.data_ref = bf16[16,48,128]{2,1,0:T(8,128)(2,1)S(1)} all-to-all(bf16[16,48,128]{2,1,0:T(8,128)(2,1)S(1)} %finish.1), channel_id=1, replica_groups=mesh['lev'=16,'lat'=64] {'lev'}, dimensions={0} | all-to-all | bytes 393216 | tf_op jit(solution)/shard_map/all_to_all | solution.py:274
  35.0 0.0 copy-done
  35.0 0.0 copy-done.1
  35.0 0.0 copy-done.2
  35.0 1.3 %physics.1 = bf16[16,48,128]{2,1,0:T(8,128)(2,1)S(1)} custom-call(bf16[16,48,128]{2,1,0:T(8,128)(2,1)S(1)} %all_to_all.10.data_ref, bf16[256,256]{1,0:T(8,128)(2,1)S(1)} %get-tuple-element.22.high_ref, bf16[256,256]{1,0:T(8,128)(2,1)S(1)} %get-tuple-element.23.low_ref, f32[192,128]{1,0:T(8,128)S(1)} %get-tuple-element.24.mask_ref, ...), custom_call_target="tpu_custom_call" | custom-call | flops 1073741824 | bytes 4194304 | tf_op jit(solution)/shard_map/physics/pallas_call | solution.py:275
  36.4 11.0 %all_to_all.11.data_ref = bf16[16,48,128]{2,1,0:T(8,128)(2,1)S(1)} all-to-all(bf16[16,48,128]{2,1,0:T(8,128)(2,1)S(1)} %physics.1), channel_id=1, replica_groups=mesh['lev'=16,'lat'=64] {'lev'}, dimensions={0} | all-to-all | bytes 393216 | tf_op jit(solution)/shard_map/all_to_all | solution.py:284
  47.4 0.8 %unpack.1 = f32[4,3,8,1024]{3,2,1,0:T(8,128)} custom-call(bf16[16,48,128]{2,1,0:T(8,128)(2,1)S(1)} %all_to_all.11.data_ref), custom_call_target="tpu_custom_call" | custom-call | flops 262144 | bytes 1048576 | tf_op jit(solution)/shard_map/unpack/pallas_call | solution.py:285
  (1 shorter events, 0.0 us)
Async XLA Ops:
  0.0 19.8 %copy-start.3 = (f32[4,8,3,1024]{3,1,2,0:T(8,128)S(1)}, f32[4,8,3,1024]{3,1,2,0:T(8,128)}, u32[]{:S(2)}) copy-start(f32[4,8,3,1024]{3,1,2,0:T(8,128)} %param.9) | copy-start | bytes 1179652
  0.0 19.8 %copy-start.4 = (f32[8,3,1024]{2,0,1:T(8,128)S(1)}, f32[8,3,1024]{2,0,1:T(8,128)}, u32[]{:S(2)}) copy-start(f32[8,3,1024]{2,0,1:T(8,128)} %param.10) | copy-start | bytes 294916
  0.0 19.8 %copy-start.5 = (f32[8,3,1024]{2,0,1:T(8,128)S(1)}, f32[8,3,1024]{2,0,1:T(8,128)}, u32[]{:S(2)}) copy-start(f32[8,3,1024]{2,0,1:T(8,128)} %param.11) | copy-start | bytes 294916
  0.0 19.8 %copy-start.6 = (f32[128,128]{1,0:T(8,128)S(1)}, f32[128,128]{1,0:T(8,128)}, u32[]{:S(2)}) copy-start(f32[128,128]{1,0:T(8,128)} %weight_ref.1) | copy-start | bytes 196612
  0.0 19.8 %copy-start.7 = (s32[1,1,8]{2,1,0:T(1,128)S(1)}, s32[1,1,8]{2,1,0:T(1,128)}, u32[]{:S(2)}) copy-start(s32[1,1,8]{2,1,0:T(1,128)} %list_ref.1) | copy-start | bytes 100
  1.1 19.6 %collective-permute-start = (bf16[5,8,1024]{2,1,0:T(8,128)(2,1)S(1)}, bf16[5,8,1024]{2,1,0:T(8,128)(2,1)S(1)}, u32[]{:S(2)}, u32[]{:S(2)}) collective-permute-start(bf16[5,8,1024]{2,1,0:T(8,128)(2,1)S(1)} %get-tuple-element.16), channel_id=1, source_target_pairs={{0,1},{2,3},{4,5},{6,7},{8,9},{10,11},{12,13},{14,15},{16,17},{18,... | collective-permute-start | bytes 245768 | tf_op jit(solution)/shard_map/ppermute | solution.py:248
  17.2 7.4 %collective-permute-start.1 = (bf16[5,8,1024]{2,1,0:T(8,128)(2,1)S(1)}, bf16[5,8,1024]{2,1,0:T(8,128)(2,1)S(1)}, u32[]{:S(2)}, u32[]{:S(2)}) collective-permute-start(bf16[5,8,1024]{2,1,0:T(8,128)(2,1)S(1)} %get-tuple-element.17), channel_id=1, source_target_pairs={{1,2},{3,4},{5,6},{7,8},{9,10},{11,12},{13,14},{15,16},{17,18},{19... | collective-permute-start | bytes 245768 | tf_op jit(solution)/shard_map/ppermute | solution.py:247
  24.6 10.5 %copy-start = (bf16[1024,1024]{1,0:T(8,128)(2,1)S(1)}, bf16[1024,1024]{1,0:T(8,128)(2,1)}, u32[]{:S(2)}) copy-start(bf16[1024,1024]{1,0:T(8,128)(2,1)} %w_mid_ref.1) | copy-start | bytes 6291460
  24.6 10.5 %copy-start.1 = (bf16[512,1024]{1,0:T(8,128)(2,1)S(1)}, bf16[512,1024]{1,0:T(8,128)(2,1)}, u32[]{:S(2)}) copy-start(bf16[512,1024]{1,0:T(8,128)(2,1)} %w_in_ref.1) | copy-start | bytes 3145732
  24.6 10.5 %copy-start.2 = (bf16[1024,512]{1,0:T(8,128)(2,1)S(1)}, bf16[1024,512]{1,0:T(8,128)(2,1)}, u32[]{:S(2)}) copy-start(bf16[1024,512]{1,0:T(8,128)(2,1)} %w_out_ref.1) | copy-start | bytes 3145732
where the time goes:
time: 48.5 us; the launch traced here: 48.2 us
  blocking collectives  21.3 us (44%)
  starting transfers between devices  17.9 us (37%)
  Pallas kernels  4.34 us (9%)
  waiting for transfers between devices  3.83 us (8%)
  between operations  0.77 us (2%)
    ppermute x1, starting transfers between devices, per_device(): near = lax.ppermute(near, 'lat', pairs(0, lat_count))  16 us
    all_to_all x1, blocking collectives, per_device(): lax.all_to_all(finished, 'lev', split_axis=0, concat_axis=0, tiled=True)  11 us
    all_to_all x1, blocking collectives, per_device(): lax.all_to_all(packed, 'lev', split_axis=0, concat_axis=0, tiled=True)  10.3 us
    ppermute x1, waiting for transfers between devices, per_device(): far = lax.ppermute(far, 'lat', pairs(1, lat_count))  3.83 us
    ppermute x1, starting transfers between devices, per_device(): far = lax.ppermute(far, 'lat', pairs(1, lat_count))  1.92 us
    pallas_call x1, Pallas kernels, per_device(): pl.pallas_call(physics_kernel, out_shape=jax.ShapeDtypeStruct(chunk, BF16...  1.35 us
    pallas_call x1, Pallas kernels, per_device(): pl.pallas_call(edge_kernel, out_shape=[jax.ShapeDtypeStruct((fields + 1,...  1.11 us
  transfers between devices with their start and end apart: 2, of which 1 were waited for; matrix products, arithmetic and copies ran while one was open for 0% of the time, Pallas kernels for 2%

commit v1 on v0

--- a/solution.py
+++ b/solution.py
@@ -107,7 +107,7 @@
     block = jnp.right_shift(column * 2731, 16)
     names = list_ref[0]
     slot = lax.broadcasted_iota(jnp.int32, names.shape, 1)
-    marks = jnp.where(slot < count_ref[:, :1], jnp.left_shift(jnp.int32(1), names), 0)
+    marks = jnp.where(slot < count_ref[0, 0], jnp.left_shift(jnp.int32(1), names), 0)
     bits = jnp.sum(marks.astype(F32), axis=1, keepdims=True).astype(jnp.int32)
     active = jnp.bitwise_and(jnp.right_shift(bits, block), 1).astype(F32)
     mask_ref[...] = active
@@ -227,6 +227,7 @@
     east = jnp.transpose(wind_east, (1, 0, 2))
     north = jnp.transpose(wind_north, (1, 0, 2))
     edge = (lev_dev, lon_cells)
+    smem = pl.BlockSpec(memory_space=pltpu.SMEM)
     hbm = pl.BlockSpec(memory_space=pltpu.HBM)
     levels = lev_dev * lev_count
     col_count = lat_rows * lon_cells // lev_count
@@ -254,12 +255,12 @@
             jax.ShapeDtypeStruct((2 * levels, 2 * levels), BF16),
             jax.ShapeDtypeStruct((col_count, 128), F32),
         ],
-        in_specs=[whole()] * 6,
+        in_specs=[whole()] * 4 + [smem, whole()],
         out_specs=[whole()] * 4,
         compiler_params=params(4),
         cost_estimate=cost(1 << 22, 1 << 22),
         name="local",
-    )(cells, east, north, block_list, lax.pad(block_count, jnp.int32(0), ((0, 0, 0), (0, 127, 0))), remap_weight)
+    )(cells, east, north, block_list, block_count, remap_weight)
     chunk = (lev_count, fields * lev_dev * lat_rows * lon_cells // lev_count // 128, 128)
     packed = pl.pallas_call(
         finish_kernel,

time: 48.5 us -> 48.4 us (level)
  no operation moved by 1% of the time
where the time goes in v1:
time: 48.4 us; the launch traced here: 48.1 us
  blocking collectives  21.2 us (44%)
  starting transfers between devices  17.9 us (37%)
  Pallas kernels  4.3 us (9%)
  waiting for transfers between devices  3.89 us (8%)
  between operations  0.76 us (2%)
    ppermute x1, starting transfers between devices, per_device(): near = lax.ppermute(near, 'lat', pairs(0, lat_count))  16 us
    all_to_all x1, blocking collectives, per_device(): lax.all_to_all(finished, 'lev', split_axis=0, concat_axis=0, tiled=True)  10.9 us
    all_to_all x1, blocking collectives, per_device(): lax.all_to_all(packed, 'lev', split_axis=0, concat_axis=0, tiled=True)  10.3 us
    ppermute x1, waiting for transfers between devices, per_device(): far = lax.ppermute(far, 'lat', pairs(1, lat_count))  3.89 us
    ppermute x1, starting transfers between devices, per_device(): far = lax.ppermute(far, 'lat', pairs(1, lat_count))  1.92 us
    pallas_call x1, Pallas kernels, per_device(): pl.pallas_call(physics_kernel, out_shape=jax.ShapeDtypeStruct(chunk, BF16...  1.35 us
    pallas_call x1, Pallas kernels, per_device(): pl.pallas_call(edge_kernel, out_shape=[jax.ShapeDtypeStruct((fields + 1,...  1.11 us
  transfers between devices with their start and end apart: 2, of which 1 were waited for; matrix products, arithmetic and copies ran while one was open for 0% of the time, Pallas kernels for 2%

profile of v1, /device:TPU:1, one launch (start us, length us, event | category | flops | bytes accessed | tf_op | source)
XLA Modules:
  0.0 48.1 jit_solution(10687896215373609791)
XLA Ops:
  0.0 0.0 copy-start.3
  0.0 0.0 copy-start.4
  0.0 0.0 copy-start.5
  0.0 0.0 copy-start.6
  0.0 0.0 copy-start.7
  0.0 1.1 %edges.1 = (bf16[5,8,1024]{2,1,0:T(8,128)(2,1)S(1)}, bf16[5,8,1024]{2,1,0:T(8,128)(2,1)S(1)}) custom-call(f32[4,3,8,1024]{3,2,1,0:T(8,128)} %bitcast.4, f32[3,8,1024]{2,1,0:T(8,128)} %bitcast.8), custom_call_target="tpu_custom_call" | custom-call | flops 8589934592 | bytes 2097152 | tf_op jit(solution)/shard_map/edges/pallas_call | solution.py:234
  1.1 16.0 %collective-permute-start = (bf16[5,8,1024]{2,1,0:T(8,128)(2,1)S(1)}, bf16[5,8,1024]{2,1,0:T(8,128)(2,1)S(1)}, u32[]{:S(2)}, u32[]{:S(2)}) collective-permute-start(bf16[5,8,1024]{2,1,0:T(8,128)(2,1)S(1)} %get-tuple-element.16), channel_id=1, source_target_pairs={{0,1},{2,3},{4,5},{6,7},{8,9},{10,11},{12,13},{14,15},{16,17},{18,... | collective-permute-start | bytes 245768 | tf_op jit(solution)/shard_map/ppermute | solution.py:249
  17.2 1.9 %collective-permute-start.1 = (bf16[5,8,1024]{2,1,0:T(8,128)(2,1)S(1)}, bf16[5,8,1024]{2,1,0:T(8,128)(2,1)S(1)}, u32[]{:S(2)}, u32[]{:S(2)}) collective-permute-start(bf16[5,8,1024]{2,1,0:T(8,128)(2,1)S(1)} %get-tuple-element.17), channel_id=1, source_target_pairs={{1,2},{3,4},{5,6},{7,8},{9,10},{11,12},{13,14},{15,16},{17,18},{19... | collective-permute-start | bytes 245768 | tf_op jit(solution)/shard_map/ppermute | solution.py:248
  19.7 0.0 copy-done.3
  19.7 0.0 copy-done.4
  19.8 0.0 copy-done.5
  19.8 0.0 copy-done.6
  19.8 0.0 copy-done.7
  19.8 0.9 %local.1 = (f32[4,3,8,1024]{3,2,1,0:T(8,128)S(1)}, bf16[256,256]{1,0:T(8,128)(2,1)S(1)}, bf16[256,256]{1,0:T(8,128)(2,1)S(1)}, f32[192,128]{1,0:T(8,128)S(1)}) custom-call(f32[4,3,8,1024]{3,2,1,0:T(8,128)S(1)} %bitcast.5, f32[3,8,1024]{2,1,0:T(8,128)S(1)} %bitcast.7, f32[3,8,1024]{2,1,0:T(8,128)S(1)} %bitcast.9, s32[1,1,8]{2,1,0:T(1,128)S(1)} %copy-done.7, ...), custom_call_target="tpu_custom_call" | custom-call | flops 4194304 | bytes 4194304 | tf_op jit(solution)/shard_map/local/pallas_call | solution.py:250
  20.7 0.0 collective-permute-done.near_ref
  20.7 3.9 %collective-permute-done.1.far_ref = bf16[5,8,1024]{2,1,0:T(8,128)(2,1)S(1)} collective-permute-done((bf16[5,8,1024]{2,1,0:T(8,128)(2,1)S(1)}, bf16[5,8,1024]{2,1,0:T(8,128)(2,1)S(1)}, u32[]{:S(2)}, u32[]{:S(2)}) %collective-permute-start.1) | collective-permute-done | bytes 81952 | tf_op jit(solution)/shard_map/ppermute | solution.py:248
  24.6 0.0 copy-start
  24.6 0.0 copy-start.1
  24.6 0.0 copy-start.2
  24.6 0.1 finish.1
  24.7 10.3 %all_to_all.10.data_ref = bf16[16,48,128]{2,1,0:T(8,128)(2,1)S(1)} all-to-all(bf16[16,48,128]{2,1,0:T(8,128)(2,1)S(1)} %finish.1), channel_id=1, replica_groups=mesh['lev'=16,'lat'=64] {'lev'}, dimensions={0} | all-to-all | bytes 393216 | tf_op jit(solution)/shard_map/all_to_all | solution.py:275
  35.0 0.0 copy-done
  35.0 0.0 copy-done.1
  35.0 0.0 copy-done.2
  35.0 1.3 %physics.1 = bf16[16,48,128]{2,1,0:T(8,128)(2,1)S(1)} custom-call(bf16[16,48,128]{2,1,0:T(8,128)(2,1)S(1)} %all_to_all.10.data_ref, bf16[256,256]{1,0:T(8,128)(2,1)S(1)} %get-tuple-element.22.high_ref, bf16[256,256]{1,0:T(8,128)(2,1)S(1)} %get-tuple-element.23.low_ref, f32[192,128]{1,0:T(8,128)S(1)} %get-tuple-element.24.mask_ref, ...), custom_call_target="tpu_custom_call" | custom-call | flops 1073741824 | bytes 4194304 | tf_op jit(solution)/shard_map/physics/pallas_call | solution.py:276
  36.4 10.9 %all_to_all.11.data_ref = bf16[16,48,128]{2,1,0:T(8,128)(2,1)S(1)} all-to-all(bf16[16,48,128]{2,1,0:T(8,128)(2,1)S(1)} %physics.1), channel_id=1, replica_groups=mesh['lev'=16,'lat'=64] {'lev'}, dimensions={0} | all-to-all | bytes 393216 | tf_op jit(solution)/shard_map/all_to_all | solution.py:285
  47.3 0.8 %unpack.1 = f32[4,3,8,1024]{3,2,1,0:T(8,128)} custom-call(bf16[16,48,128]{2,1,0:T(8,128)(2,1)S(1)} %all_to_all.11.data_ref), custom_call_target="tpu_custom_call" | custom-call | flops 262144 | bytes 1048576 | tf_op jit(solution)/shard_map/unpack/pallas_call | solution.py:286
Async XLA Ops:
  0.0 19.7 %copy-start.3 = (f32[4,8,3,1024]{3,1,2,0:T(8,128)S(1)}, f32[4,8,3,1024]{3,1,2,0:T(8,128)}, u32[]{:S(2)}) copy-start(f32[4,8,3,1024]{3,1,2,0:T(8,128)} %param.9) | copy-start | bytes 1179652
  0.0 19.7 %copy-start.4 = (f32[8,3,1024]{2,0,1:T(8,128)S(1)}, f32[8,3,1024]{2,0,1:T(8,128)}, u32[]{:S(2)}) copy-start(f32[8,3,1024]{2,0,1:T(8,128)} %param.10) | copy-start | bytes 294916
  0.0 19.8 %copy-start.5 = (f32[8,3,1024]{2,0,1:T(8,128)S(1)}, f32[8,3,1024]{2,0,1:T(8,128)}, u32[]{:S(2)}) copy-start(f32[8,3,1024]{2,0,1:T(8,128)} %param.11) | copy-start | bytes 294916
  0.0 19.8 %copy-start.6 = (f32[128,128]{1,0:T(8,128)S(1)}, f32[128,128]{1,0:T(8,128)}, u32[]{:S(2)}) copy-start(f32[128,128]{1,0:T(8,128)} %weight_ref.1) | copy-start | bytes 196612
  0.0 19.8 %copy-start.7 = (s32[1,1,8]{2,1,0:T(1,128)S(1)}, s32[1,1,8]{2,1,0:T(1,128)}, u32[]{:S(2)}) copy-start(s32[1,1,8]{2,1,0:T(1,128)} %list_ref.1) | copy-start | bytes 100
  1.1 19.5 %collective-permute-start = (bf16[5,8,1024]{2,1,0:T(8,128)(2,1)S(1)}, bf16[5,8,1024]{2,1,0:T(8,128)(2,1)S(1)}, u32[]{:S(2)}, u32[]{:S(2)}) collective-permute-start(bf16[5,8,1024]{2,1,0:T(8,128)(2,1)S(1)} %get-tuple-element.16), channel_id=1, source_target_pairs={{0,1},{2,3},{4,5},{6,7},{8,9},{10,11},{12,13},{14,15},{16,17},{18,... | collective-permute-start | bytes 245768 | tf_op jit(solution)/shard_map/ppermute | solution.py:249
  17.2 7.4 %collective-permute-start.1 = (bf16[5,8,1024]{2,1,0:T(8,128)(2,1)S(1)}, bf16[5,8,1024]{2,1,0:T(8,128)(2,1)S(1)}, u32[]{:S(2)}, u32[]{:S(2)}) collective-permute-start(bf16[5,8,1024]{2,1,0:T(8,128)(2,1)S(1)} %get-tuple-element.17), channel_id=1, source_target_pairs={{1,2},{3,4},{5,6},{7,8},{9,10},{11,12},{13,14},{15,16},{17,18},{19... | collective-permute-start | bytes 245768 | tf_op jit(solution)/shard_map/ppermute | solution.py:248
  24.6 10.5 %copy-start = (bf16[1024,1024]{1,0:T(8,128)(2,1)S(1)}, bf16[1024,1024]{1,0:T(8,128)(2,1)}, u32[]{:S(2)}) copy-start(bf16[1024,1024]{1,0:T(8,128)(2,1)} %w_mid_ref.1) | copy-start | bytes 6291460
  24.6 10.5 %copy-start.1 = (bf16[512,1024]{1,0:T(8,128)(2,1)S(1)}, bf16[512,1024]{1,0:T(8,128)(2,1)}, u32[]{:S(2)}) copy-start(bf16[512,1024]{1,0:T(8,128)(2,1)} %w_in_ref.1) | copy-start | bytes 3145732
  24.6 10.5 %copy-start.2 = (bf16[1024,512]{1,0:T(8,128)(2,1)S(1)}, bf16[1024,512]{1,0:T(8,128)(2,1)}, u32[]{:S(2)}) copy-start(bf16[1024,512]{1,0:T(8,128)(2,1)} %w_out_ref.1) | copy-start | bytes 3145732
